TPU v7x, 32 devices: a whole 2x2x4 slice. The times are simulated.
32 devices in a mesh: shard: 4 (over y, x), rep: 8 (over z, core).
Axes of the slice: x: 2, y: 2, z: 4, core: 2. Of those that a mesh axis runs over, the one named last changes fastest.
Arguments:
- tokens: bfloat16 [16384, 8192], P('rep', 'shard'), may hold values from -21 to 21
- key_cotangent: bfloat16 [16384, 1024], P('rep'), may hold values from -21 to 21
- value_cotangent: bfloat16 [16384, 1024], P('rep'), may hold values from -21 to 21
- key_weight: float32 [8192, 1024], P(('shard', 'rep')), may hold values from -0.75 to 0.75
- value_weight: float32 [8192, 1024], P(('shard', 'rep')), may hold values from -0.75 to 0.75
- key_moment: float32 [8192, 1024], P(('shard', 'rep')), may hold values from -6 to 6
- value_moment: float32 [8192, 1024], P(('shard', 'rep')), may hold values from -6 to 6
Outputs:
- new_key_weight: float32 [8192, 1024], P(('shard', 'rep'))
- new_value_weight: float32 [8192, 1024], P(('shard', 'rep'))
- new_key_moment: float32 [8192, 1024], P(('shard', 'rep'))
- new_value_moment: float32 [8192, 1024], P(('shard', 'rep'))
All inputs are finite; a program needn't handle non-finite values.
Results may differ from a plain program's by a relative error of at most 0.0003.
Values may be sent and summed in bfloat16 or wider, within the bound.
A program may use at most 128 MiB of HBM per device.

v0:
```python
import functools
import math

import jax
import jax.numpy as jnp
from jax import lax
from jax.experimental import pallas as pl
from jax.experimental.pallas import tpu as pltpu
from jax.sharding import PartitionSpec as P

EPSILON = 1e-06
MOMENTUM_DECAY = 0.9
STEP_SIZE = 0.01
TINY_BOUND = 1e-16
TOP = 32768.0
FLOOR = 2.0**-120
CODE = jnp.bfloat16
MESH = pl.DeviceIdType.MESH
LANES = 128
ROWS = 16
PARTS = 4


def pair_coefs(cross, first_square, second_square):
    first = 1.0 - cross / (2.0 * (first_square + EPSILON))
    second = 1.0 - cross / (2.0 * (second_square + EPSILON))
    return first, second


def tree_coefs(gram):
    count = len(gram)
    coefs = [1.0] * count
    span = 1
    while len(gram) > 1:
        pairs = [
            pair_coefs(gram[i][i + 1], gram[i][i], gram[i + 1][i + 1])
            for i in range(0, len(gram), 2)
        ]
        for member in range(count):
            coefs[member] = coefs[member] * pairs[member // (2 * span)][member // span % 2]
        half = len(gram) // 2
        merged = [[None] * half for _ in range(half)]
        for i in range(half):
            for j in range(half):
                merged[i][j] = sum(
                    pairs[i][a] * pairs[j][b] * gram[2 * i + a][2 * j + b]
                    for a in range(2)
                    for b in range(2)
                )
        gram = merged
        span *= 2
    return coefs


def norm_bound(coefs, squares):
    bound = jnp.abs(coefs[0]) * jnp.sqrt(squares[0]) + jnp.abs(coefs[1]) * jnp.sqrt(squares[1])
    return jnp.maximum(bound, TINY_BOUND)


def sided(is_first, own, other):
    return jnp.where(is_first, own, other), jnp.where(is_first, other, own)


def encode(value):
    power = value * value
    power = power * power
    power = power * power
    return jnp.where(value < 0.0, -power, power).astype(CODE)


def decode(coded):
    coded = coded.astype(jnp.float32)
    fourth = lax.rsqrt(lax.rsqrt(jnp.maximum(jnp.abs(coded), FLOOR)))
    eighth = fourth * lax.rsqrt(fourth)
    return jnp.where(coded > 0.0, eighth, jnp.where(coded < 0.0, -eighth, 0.0))


def fold(product):
    total = jnp.sum(product.reshape(-1, 8, product.shape[-1]), axis=0)
    return sum(total[:, i : i + LANES] for i in range(0, total.shape[1], LANES))


def scalar(tile):
    return jnp.sum(jnp.sum(tile, axis=0, keepdims=True), axis=1, keepdims=True)


class Exchange:
    def __init__(self, span, shard_count, rep, shard, payload, inbox, send_sem, recv_sem):
        self.span, self.shard_count, self.rep, self.shard = span, shard_count, rep, shard
        self.payload, self.inbox = payload, inbox
        self.send_sem, self.recv_sem = send_sem, recv_sem
        self.shape = payload.shape

    def copy(self, slot):
        inside = lax.rem(self.rep, self.span)
        near, far = lax.rem(slot, self.span), lax.div(slot, self.span)
        target = self.rep - inside + lax.rem(inside + near, self.span)
        return pltpu.make_async_remote_copy(
            src_ref=self.payload,
            dst_ref=self.inbox.at[slot],
            send_sem=self.send_sem.at[slot],
            recv_sem=self.recv_sem.at[slot],
            device_id=(lax.rem(self.shard + far, self.shard_count), target),
            device_id_type=MESH,
        )

    def start(self, placed):
        flat = lax.broadcasted_iota(jnp.int32, self.shape, 0) * LANES
        flat = flat + lax.broadcasted_iota(jnp.int32, self.shape, 1)
        tile = jnp.zeros(self.shape, jnp.float32)
        for place, value in placed:
            tile = jnp.where(flat == place, value, tile)
        self.payload[...] = tile

        @pl.loop(1, self.span * self.shard_count)
        def _(slot):
            self.copy(slot).start()

    def finish(self):
        @pl.loop(1, self.span * self.shard_count)
        def _(slot):
            self.copy(slot).wait()

        total = self.payload[...]
        for slot in range(1, self.span * self.shard_count):
            total = total + self.inbox[slot]
        return lambda place: total[
            place // LANES : place // LANES + 1, place % LANES : place % LANES + 1
        ]


def owns(rep, shard, members):
    return (shard == 0) & (lax.rem(rep, members) == 0)


def final_places(sums, count, size, base, scale, rep, shard):
    unit = lax.div(rep, size)
    for (i, j), value in sums:
        left = lax.rem(unit - i + count, count)
        right = lax.rem(unit - j + count, count)
        yield base + jnp.minimum(left, right) * count + jnp.maximum(left, right), value
    yield base + count * count + unit, jnp.where(owns(rep, shard, size), scale, 0.0)


def final_weights(read, count, size, base, rep):
    unit = lax.div(rep, size)
    scales = [read(base + count * count + i) for i in range(count)]
    gram = [[None] * count for _ in range(count)]
    for i in range(count):
        for j in range(i, count):
            gram[i][j] = read(base + i * count + j) * (scales[i] * scales[j])
            gram[j][i] = gram[i][j]
    weights = [coef * scale for coef, scale in zip(tree_coefs(gram), scales)]
    for step in range(count):
        source = lax.rem(unit - step + count, count)
        chosen = weights[0]
        for i in range(1, count):
            chosen = jnp.where(source == i, weights[i], chosen)
        yield chosen


def merge_kernel(replicas, shard_count, *refs):
    (tokens_hbm, key_hbm, value_hbm, params_hbm) = refs[0], refs[1], refs[2], refs[3:7]
    outs = refs[7:11]
    (
        tokens, cotangents, key_full, value_full, key_other, value_other,
        key_send, key_recv, half_send, half_recv, last_send, last_recv,
        params, held,
        key_pay, key_in, value_pay, value_in, duo_pay, duo_in, final_pay, final_in,
        token_sem, load_sem, swap_send, swap_recv,
        key_ss, key_rs, half_ss, half_rs, last_ss, last_rs,
        kx_s, kx_r, vx_s, vx_r, dx_s, dx_r, fx_s, fx_r,
    ) = refs[11:]
    rep, shard = lax.axis_index("rep"), lax.axis_index("shard")
    groups, duos = replicas // 2, replicas // 4
    core, group = lax.rem(rep, 2), lax.div(rep, 2)
    half, duo = lax.rem(group, 2), lax.div(group, 2)
    block, features = key_other.shape[1], key_other.shape[2]
    factor = 1.0 / math.sqrt(tokens.shape[0])
    barrier = pltpu.get_barrier_semaphore()

    @pl.loop(1, replicas * shard_count)
    def _(slot):
        peer = (
            lax.rem(shard + lax.div(slot, replicas), shard_count),
            lax.rem(rep + lax.rem(slot, replicas), replicas),
        )
        pl.semaphore_signal(barrier, inc=1, device_id=peer, device_id_type=MESH)

    def remote(source, target, send_sem, recv_sem, peer):
        return pltpu.make_async_remote_copy(
            src_ref=source, dst_ref=target, send_sem=send_sem, recv_sem=recv_sem,
            device_id=(shard, peer), device_id_type=MESH,
        )

    unit = 2 * block

    def token_copy(j):
        columns = pl.ds(pl.multiple_of(j * unit, unit), unit)
        return pltpu.make_async_copy(
            tokens_hbm.at[:, columns], tokens.at[:, columns], token_sem.at[j]
        )

    loads = [
        pltpu.make_async_copy(key_hbm, cotangents.at[0], load_sem.at[0]),
        pltpu.make_async_copy(value_hbm, cotangents.at[1], load_sem.at[1]),
    ]
    loads += [
        pltpu.make_async_copy(source, params.at[i], load_sem.at[2 + i])
        for i, source in enumerate(params_hbm)
    ]
    loads[0].start()
    for j in range(groups):
        token_copy(j).start()
    for load in loads[1:]:
        load.start()

    def swap(which, j):
        full, other = (key_full, key_other) if which == 0 else (value_full, value_other)
        return remote(
            full.at[j, 1 - core], other.at[j], swap_send.at[which, j], swap_recv.at[which, j],
            rep + 1 - 2 * core,
        )

    def multiply(which, j):
        full = key_full if which == 0 else value_full
        left = tokens[:, pl.ds(pl.multiple_of(j * unit, unit), unit)]
        width = min(features, 512)
        for at in range(0, features, width):
            product = lax.dot_general(
                left, cotangents[which, :, at : at + width], (((0,), (0,)), ((), ())),
                preferred_element_type=jnp.float32,
            ) * factor
            full[j, 0, :, at : at + width] = product[:block]
            full[j, 1, :, at : at + width] = product[block:]

    def rows(i, size=ROWS):
        return pl.ds(pl.multiple_of(i * size, size), size)

    zero = jnp.zeros((8, LANES), jnp.float32)

    def duel(pairs, sums):
        for own, other in pairs:
            def body(i, carry, own=own, other=other):
                left, right = own(rows(i)), other(rows(i))
                cross, first, second = carry
                return (
                    cross + fold(left * right),
                    first + fold(left * left),
                    second + fold(right * right),
                )
            sums = lax.fori_loop(0, block // ROWS, body, sums)
        return sums

    def pair_sums(which):
        full, other = (key_full, key_other) if which == 0 else (value_full, value_other)

        def body(j, sums):
            swap(which, j).wait_recv()
            return duel([(lambda r: full[j, core, r, :], lambda r: other[j, r, :])], sums)

        return [scalar(tile) for tile in lax.fori_loop(0, groups, body, (zero,) * 3)]

    def pair_places(sums, is_first):
        first, second = sided(is_first, sums[1], sums[2])
        return [(0, sums[0]), (1, first), (2, second)]

    def pair_finish(read):
        squares = (read(1), read(2))
        first, second = pair_coefs(read(0), *squares)
        scale = norm_bound((first, second), squares) / TOP
        own, other = sided(core == 0, first / scale, second / scale)
        return own, other, scale

    def hold(at, values):
        for i, value in enumerate(values):
            held[at + i : at + i + 1, :] = jnp.broadcast_to(value, (1, LANES))

    def holds(at, count):
        return [held[at + i : at + i + 1, 0:1] for i in range(count)]

    def around(span, *scratch):
        return Exchange(span, shard_count, rep, shard, *scratch)

    key_exchange = around(2, key_pay, key_in, kx_s, kx_r)
    value_exchange = around(2, value_pay, value_in, vx_s, vx_r)
    duo_exchange = around(4, duo_pay, duo_in, dx_s, dx_r)
    final_exchange = around(replicas, final_pay, final_in, fx_s, fx_r)

    part = block // PARTS

    def key_copy(step, q):
        target = lax.rem(group + step, groups)
        place = pl.ds(q * part, part)
        return remote(
            key_send.at[step - 1, place], key_recv.at[step - 1, place],
            key_ss.at[step - 1, q], key_rs.at[step - 1, q], 2 * target + core,
        )

    def key_encode(step):
        own, other = holds(0, 2)
        target = lax.rem(group + step, groups)

        @pl.loop(0, block // ROWS)
        def _(i):
            r = rows(i)
            key_send[step - 1, r, :] = encode(
                own * key_full[target, core, r, :] + other * key_other[target, r, :]
            )

    def half_copy(d):
        return remote(
            half_send.at[d], half_recv.at[d], half_ss.at[d], half_rs.at[d],
            rep + 2 - 4 * half,
        )

    def last_copy(step):
        target = lax.rem(duo + step, duos)
        return remote(
            last_send.at[step - 1], last_recv.at[step - 1],
            last_ss.at[step - 1], last_rs.at[step - 1], rep + 4 * (target - duo),
        )

    first_steps = [groups - 1]
    last_steps = [1]
    middle_steps = list(range(groups - 2, 1, -1))

    @pl.loop(0, groups)
    def _(j):
        token_copy(j).wait()

        @pl.when(j == 0)
        def _():
            loads[0].wait()

        multiply(0, j)

        @pl.when(j == 0)
        def _():
            pl.semaphore_wait(barrier, replicas * shard_count - 1)

        swap(0, j).start()

    key_exchange.start(pair_places(pair_sums(0), core == 0))
    loads[1].wait()

    @pl.loop(0, groups)
    def _(j):
        @pl.when(j == 1)
        def _():
            hold(0, pair_finish(key_exchange.finish()))
            for step in first_steps:
                key_encode(step)
                for q in range(PARTS):
                    key_copy(step, q).start()
            for step in middle_steps + last_steps:
                key_encode(step)
            key_copy(1, 0).start()

        multiply(1, j)
        swap(1, j).start()

    value_exchange.start(pair_places(pair_sums(1), core == 0))

    key_blocks = key_other
    own, other, key_scale = holds(0, 3)

    @pl.loop(0, block // ROWS)
    def _(i):
        r = rows(i)
        key_blocks[0, r, :] = own * key_full[group, core, r, :] + other * key_other[group, r, :]

    own, other, value_scale = pair_finish(value_exchange.finish())
    hold(3, (own, other, value_scale))
    for d in range(duos):
        @pl.loop(0, block // ROWS)
        def _(i):
            r, j = rows(i), 2 * d + 1 - half
            half_send[d, r, :] = encode(
                own * value_full[j, core, r, :] + other * value_other[j, r, :]
            )

        half_copy(d).start()
    for step in middle_steps:
        key_copy(step, 0).start()
    own, other = holds(3, 2)
    for d in range(duos):
        @pl.loop(0, block // ROWS)
        def _(i):
            r, j = rows(i), 2 * d + half
            value_other[j, r, :] = own * value_full[j, core, r, :] + other * value_other[j, r, :]

    def absorb(read, blocks, slot, ready, sums, begin, size):
        mine = sorted(ready) + [slot]

        def body(i, carry):
            r = rows(i)
            value = read(r)
            blocks(slot, r, value)
            others = [blocks(b, r) for b in mine[:-1]] + [value]
            return tuple(c + fold(value * o) for c, o in zip(carry, others))

        stop = (begin + size) // ROWS
        start = tuple(
            sums.get((min(slot, b), max(slot, b)), zero) for b in mine
        )
        done = lax.fori_loop(begin // ROWS, stop, body, start)
        for b, tile in zip(mine, done):
            sums[(min(slot, b), max(slot, b))] = tile

    def key_access(slot, r, value=None):
        if value is None:
            return key_blocks[slot, r, :]
        key_blocks[slot, r, :] = value

    def value_access(slot, r, value=None):
        if value is None:
            return value_full[slot, 0, r, :]
        value_full[slot, 0, r, :] = value

    key_sums, value_sums, key_ready, value_ready = {}, {}, [], []

    def absorb_own_key():
        def body(i, carry):
            value = key_blocks[0, rows(i), :]
            return carry + fold(value * value)
        key_sums[(0, 0)] = lax.fori_loop(0, block // ROWS, body, zero)
        key_ready.append(0)

    def absorb_key(step):
        for q in range(PARTS):
            key_copy(step, q).wait_recv()
            absorb(
                lambda r: decode(key_recv[step - 1, r, :]), key_access, step, key_ready,
                key_sums, q * part, part,
            )
        key_ready.append(step)

    absorb_own_key()
    for step in first_steps:
        absorb_key(step)

    for d in range(duos):
        half_copy(d).wait_recv()

        def body(i, carry, d=d):
            r = rows(i)
            left = value_other[2 * d + half, r, :]
            right = decode(half_recv[d, r, :])
            value_other[2 * d + 1 - half, r, :] = right
            cross, first, second = carry
            return (
                cross + fold(left * right),
                first + fold(left * left),
                second + fold(right * right),
            )

        duo_sums = lax.fori_loop(
            0, block // ROWS, body, (zero,) * 3 if d == 0 else duo_sums
        )
    even = half == 0
    places = pair_places([scalar(tile) for tile in duo_sums], even)
    mine = jnp.where(owns(rep, shard, 2), value_scale, 0.0)
    low, high = sided(even, mine, jnp.zeros_like(mine))
    duo_exchange.start(places + [(3, low), (4, high)])
    for step in middle_steps:
        for q in range(1, PARTS):
            key_copy(step, q).start()
    for j in range(groups):
        swap(1, j).wait_send()
    read = duo_exchange.finish()
    low, high = read(3), read(4)
    squares = (read(1) * (low * low), read(2) * (high * high))
    first, second = pair_coefs(read(0) * (low * high), *squares)
    duo_scale = norm_bound((first, second), squares) / TOP
    own, other = sided(even, first * low / duo_scale, second * high / duo_scale)

    def duo_block(target, r):
        return (
            own * value_other[2 * target + half, r, :]
            + other * value_other[2 * target + 1 - half, r, :]
        )

    for step in range(1, duos):
        @pl.loop(0, block // ROWS)
        def _(i):
            r = rows(i)
            last_send[step - 1, r, :] = encode(duo_block(lax.rem(duo + step, duos), r))

        last_copy(step).start()
    for step in last_steps:
        for q in range(1, PARTS):
            key_copy(step, q).start()
    absorb(
        lambda r: duo_block(duo, r), value_access, 0, value_ready, value_sums, 0, block
    )
    value_ready.append(0)
    for step in middle_steps:
        absorb_key(step)
    for step in range(1, duos):
        last_copy(step).wait_recv()
        absorb(
            lambda r: decode(last_recv[step - 1, r, :]), value_access, step, value_ready,
            value_sums, 0, block,
        )
        value_ready.append(step)
    for step in last_steps:
        absorb_key(step)

    key_base, value_base = 0, groups * (groups + 1)
    key_places = [(pair, scalar(tile)) for pair, tile in key_sums.items()]
    value_places = [(pair, scalar(tile)) for pair, tile in value_sums.items()]
    places = list(final_places(key_places, groups, 2, key_base, key_scale, rep, shard))
    places += list(final_places(value_places, duos, 4, value_base, duo_scale, rep, shard))
    final_exchange.start(places)
    for j in range(groups):
        swap(0, j).wait_send()
    for step in range(1, groups):
        for q in range(PARTS):
            key_copy(step, q).wait_send()
    for d in range(duos):
        half_copy(d).wait_send()
    for step in range(1, duos):
        last_copy(step).wait_send()
    for load in loads[2:]:
        load.wait()
    read = final_exchange.finish()
    key_weights = list(final_weights(read, groups, 2, key_base, rep))
    value_weights = list(final_weights(read, duos, 4, value_base, rep))

    @pl.loop(0, block // 8)
    def _(i):
        r = rows(i, 8)
        key_merged = sum(w * key_blocks[b, r, :] for b, w in enumerate(key_weights))
        value_merged = sum(w * value_full[b, 0, r, :] for b, w in enumerate(value_weights))
        for which, merged in enumerate((key_merged, value_merged)):
            moment = MOMENTUM_DECAY * params[2 + which, r, :] + merged
            outs[2 + which][r, :] = moment
            outs[which][r, :] = params[which, r, :] - STEP_SIZE * moment


def shards(
    tokens, key_cotangent, value_cotangent, key_weight, value_weight, key_moment, value_moment
):
    replicas, shard_count = lax.axis_size("rep"), lax.axis_size("shard")
    depth, width = tokens.shape
    features = key_cotangent.shape[1]
    groups, duos = replicas // 2, replicas // 4
    block = width // replicas
    f32, dma = jnp.float32, pltpu.SemaphoreType.DMA
    entries = groups * (groups + 1) + duos * (duos + 1)
    lines = -(-entries // LANES)

    def small(span, lines=1):
        return [
            pltpu.VMEM((lines, LANES), f32),
            pltpu.VMEM((span * shard_count, lines, LANES), f32),
        ]

    def coded(count):
        return [pltpu.VMEM((max(count, 1), block, features), CODE)] * 2

    def pair(*shape):
        return [dma(shape)] * 2

    scratch = [
        pltpu.VMEM((depth, width), tokens.dtype),
        pltpu.VMEM((2, depth, features), key_cotangent.dtype),
        pltpu.VMEM((groups, 2, block, features), f32),
        pltpu.VMEM((groups, 2, block, features), f32),
        pltpu.VMEM((groups, block, features), f32),
        pltpu.VMEM((groups, block, features), f32),
        *coded(groups - 1), *coded(duos), *coded(duos - 1),
        pltpu.VMEM((4, block, features), f32),
        pltpu.VMEM((8, LANES), f32),
        *small(2), *small(2), *small(4), *small(replicas, lines),
        dma((groups,)), dma((6,)), *pair(2, groups),
        *pair(groups - 1, PARTS), *pair(duos), *pair(max(duos - 1, 1)),
        *pair(2 * shard_count), *pair(2 * shard_count), *pair(4 * shard_count),
        *pair(replicas * shard_count),
    ]
    row = jax.ShapeDtypeStruct((block, features), f32)
    return pl.pallas_call(
        functools.partial(merge_kernel, replicas, shard_count),
        out_shape=[row] * 4,
        in_specs=[pl.BlockSpec(memory_space=pl.ANY)] * 7,
        out_specs=[pl.BlockSpec(memory_space=pltpu.VMEM)] * 4,
        scratch_shapes=scratch,
        compiler_params=pltpu.CompilerParams(
            collective_id=0, has_side_effects=True, vmem_limit_bytes=62 * 2**20
        ),
    )(
        tokens, key_cotangent, value_cotangent, key_weight, value_weight, key_moment, value_moment
    )


def solution(mesh):
    grads = (P("rep", None),) * 2
    rows = (P(("shard", "rep"), None),) * 4
    return jax.shard_map(
        shards, mesh=mesh, in_specs=(P("rep", "shard"),) + grads + rows, out_specs=rows,
        check_vma=False,
    )
```

profile of v0, /device:TPU:0, one launch (start us, length us, event | category | flops | bytes accessed | tf_op | source)
XLA Modules:
  0.0 136.2 jit_solution(15729645131107736466)
XLA Ops:
  0.6 128.9 %shard_map.102 = (f32[256,1024]{1,0:T(8,128)}, f32[256,1024]{1,0:T(8,128)}, f32[256,1024]{1,0:T(8,128)}, f32[256,1024]{1,0:T(8,128)}) custom-call(bf16[2048,2048]{1,0:T(8,128)(2,1)} %refs_0_.1, bf16[2048,1024]{1,0:T(8,128)(2,1)} %refs_1_.1, bf16[2048,1024]{1,0:T(8,128)(2,1)} %refs_2_.1, f32[256,1024]{1,0:T(8,128)} %refs_3_.1, f32[256,1024]{1,0:T(8,128)} %refs_4_.1, ...), custom_call_target="tpu_custom_call" | custom-call | tf_op jit(solution)/shard_map/pallas_call | solution.py:583
  129.5 0.0 copy-start.1
  129.5 0.0 copy-start
  129.5 2.5 %copy.15 = f32[256,1024]{1,0:T(8,128)} copy(f32[256,1024]{1,0:T(8,128)} %get-tuple-element.8) | data formatting | bytes 2097152
  132.0 2.3 %copy.16 = f32[256,1024]{1,0:T(8,128)} copy(f32[256,1024]{1,0:T(8,128)} %get-tuple-element.9) | data formatting | bytes 2097152
  134.3 0.0 copy-done.1
  134.3 1.0 copy.17
  135.3 0.0 copy-done
  135.3 1.0 copy.18
Async XLA Ops:
  129.5 4.8 %copy-start.1 = (f32[256,1024]{1,0:T(8,128)S(1)}, f32[256,1024]{1,0:T(8,128)}, u32[]{:S(2)}) copy-start(f32[256,1024]{1,0:T(8,128)} %get-tuple-element.10) | copy-start | bytes 3145732
  129.5 5.7 %copy-start = (f32[256,1024]{1,0:T(8,128)S(1)}, f32[256,1024]{1,0:T(8,128)}, u32[]{:S(2)}) copy-start(f32[256,1024]{1,0:T(8,128)} %get-tuple-element.11) | copy-start | bytes 3145732
where the time goes:
time: 136 us
  Pallas kernels  129 us (95%)
  local copies, waits for them, and re-layouts  6.71 us (5%)
    pallas_call x1, Pallas kernels, shards(): pl.pallas_call(functools.partial(merge_kernel, replicas, shard_count), ou...  129 us
    unnamed x8, local copies, waits for them, and re-layouts  6.71 us

commit v1 on v0

v1 whole, which is shorter than its diff:
```python
import functools
import math

import jax
import jax.numpy as jnp
from jax import lax
from jax.experimental import pallas as pl
from jax.experimental.pallas import tpu as pltpu
from jax.sharding import PartitionSpec as P

EPSILON = 1e-06
MOMENTUM_DECAY = 0.9
STEP_SIZE = 0.01
TINY_BOUND = 1e-16
TOP = 32768.0
FLOOR = 2.0**-120
CODE = jnp.bfloat16
MESH = pl.DeviceIdType.MESH
LANES = 128
ROWS = 32
PARTS = 4
BUNCHES = 4
SPLITS = 2
EARLY = 0
BEHIND = 3
RAW = 2
VMEM_LIMIT = 54 * 2**20


def pair_coefs(cross, first_square, second_square):
    first = 1.0 - cross / (2.0 * (first_square + EPSILON))
    second = 1.0 - cross / (2.0 * (second_square + EPSILON))
    return first, second


def tree_coefs(gram):
    count = len(gram)
    coefs = [1.0] * count
    span = 1
    while len(gram) > 1:
        pairs = [
            pair_coefs(gram[i][i + 1], gram[i][i], gram[i + 1][i + 1])
            for i in range(0, len(gram), 2)
        ]
        for member in range(count):
            coefs[member] = coefs[member] * pairs[member // (2 * span)][member // span % 2]
        half = len(gram) // 2
        merged = [[None] * half for _ in range(half)]
        for i in range(half):
            for j in range(half):
                merged[i][j] = sum(
                    pairs[i][a] * pairs[j][b] * gram[2 * i + a][2 * j + b]
                    for a in range(2)
                    for b in range(2)
                )
        gram = merged
        span *= 2
    return coefs


def norm_bound(coefs, squares):
    bound = jnp.abs(coefs[0]) * jnp.sqrt(squares[0]) + jnp.abs(coefs[1]) * jnp.sqrt(squares[1])
    return jnp.maximum(bound, TINY_BOUND)


def sided(is_first, own, other):
    return jnp.where(is_first, own, other), jnp.where(is_first, other, own)


def encode(value):
    power = value * value
    power = power * power
    power = power * power
    return jnp.where(value < 0.0, -power, power).astype(CODE)


def decode(coded):
    coded = coded.astype(jnp.float32)
    fourth = lax.rsqrt(lax.rsqrt(jnp.maximum(jnp.abs(coded), FLOOR)))
    eighth = fourth * lax.rsqrt(fourth)
    return jnp.where(coded > 0.0, eighth, jnp.where(coded < 0.0, -eighth, 0.0))


def tree_sum(terms):
    while len(terms) > 1:
        terms = [sum(terms[i : i + 2]) for i in range(0, len(terms), 2)]
    return terms[0]


def fold(product):
    return tree_sum([
        product[i : i + 8, j : j + LANES]
        for i in range(0, product.shape[0], 8)
        for j in range(0, product.shape[1], LANES)
    ])


def scalar(tile):
    return jnp.sum(jnp.sum(tile, axis=0, keepdims=True), axis=1, keepdims=True)


class Exchange:
    def __init__(self, span, shard_count, rep, shard, payload, inbox, send_sem, recv_sem):
        self.span, self.shard_count, self.rep, self.shard = span, shard_count, rep, shard
        self.payload, self.inbox = payload, inbox
        self.send_sem, self.recv_sem = send_sem, recv_sem
        self.shape = payload.shape

    def copy(self, slot):
        inside = lax.rem(self.rep, self.span)
        near, far = lax.rem(slot, self.span), lax.div(slot, self.span)
        target = self.rep - inside + lax.rem(inside + near, self.span)
        return pltpu.make_async_remote_copy(
            src_ref=self.payload,
            dst_ref=self.inbox.at[slot],
            send_sem=self.send_sem.at[slot],
            recv_sem=self.recv_sem.at[slot],
            device_id=(lax.rem(self.shard + far, self.shard_count), target),
            device_id_type=MESH,
        )

    def start(self, placed):
        flat = lax.broadcasted_iota(jnp.int32, self.shape, 0) * LANES
        flat = flat + lax.broadcasted_iota(jnp.int32, self.shape, 1)
        tile = jnp.zeros(self.shape, jnp.float32)
        for place, value in placed:
            tile = jnp.where(flat == place, value, tile)
        self.payload[...] = tile

        @pl.loop(1, self.span * self.shard_count)
        def _(slot):
            self.copy(slot).start()

    def finish(self):
        @pl.loop(1, self.span * self.shard_count)
        def _(slot):
            self.copy(slot).wait()

        total = self.payload[...]
        for slot in range(1, self.span * self.shard_count):
            total = total + self.inbox[slot]

        def read(place):
            line, lane = place // LANES, place % LANES
            row = total[line : line + 1, :]
            return (pltpu.roll(row, LANES - lane, 1) if lane else row)[:, :1]

        return read


def owns(rep, shard, members):
    return (shard == 0) & (lax.rem(rep, members) == 0)


def final_places(sums, count, size, base, scale, rep, shard, offset):
    unit = lax.div(rep, size)
    for (i, j), value in sums:
        left = lax.rem(unit - offset(i) + count, count)
        right = lax.rem(unit - offset(j) + count, count)
        yield base + jnp.minimum(left, right) * count + jnp.maximum(left, right), value
    yield base + count * count + unit, jnp.where(owns(rep, shard, size), scale, 0.0)


def final_weights(read, count, size, base, rep, offset):
    unit = lax.div(rep, size)
    scales = [read(base + count * count + i) for i in range(count)]
    gram = [[None] * count for _ in range(count)]
    for i in range(count):
        for j in range(i, count):
            gram[i][j] = read(base + i * count + j) * (scales[i] * scales[j])
            gram[j][i] = gram[i][j]
    weights = [coef * scale for coef, scale in zip(tree_coefs(gram), scales)]
    for slot in range(count):
        source = lax.rem(unit - offset(slot) + count, count)
        chosen = weights[0]
        for i in range(1, count):
            chosen = jnp.where(source == i, weights[i], chosen)
        yield chosen


def merge_kernel(replicas, shard_count, *refs):
    tokens_hbm, key_hbm, value_hbm = refs[:3]
    key_out, value_out = refs[3:5]
    (
        tokens, cotangents, key_full, value_full, key_other, value_other,
        key_send, key_recv, half_send, half_recv, last_send, last_recv, raw_send, raw_recv,
        held, wide, raw_pay, raw_in,
        key_pay, key_in, value_pay, value_in, duo_pay, duo_in, final_pay, final_in,
        token_sem, load_sem, swap_send, swap_recv,
        key_ss, key_rs, half_ss, half_rs, last_ss, last_rs, raw_ss, raw_rs, rw_s, rw_r,
        kx_s, kx_r, vx_s, vx_r, dx_s, dx_r, fx_s, fx_r,
    ) = refs[5:]
    rep, shard = lax.axis_index("rep"), lax.axis_index("shard")
    groups, duos = replicas // 2, replicas // 4
    core, group = lax.rem(rep, 2), lax.div(rep, 2)
    half, duo = lax.rem(group, 2), lax.div(group, 2)
    block, features = key_other.shape[1], key_other.shape[2]
    width = features // SPLITS
    factor = 1.0 / math.sqrt(tokens.shape[0])
    size = min(block, ROWS)
    parts = min(PARTS, block // 16)
    part = block // parts
    barrier = pltpu.get_barrier_semaphore()

    forward = group < duos
    inner = (half == 1) == forward
    outer = jnp.logical_not(inner)

    def key_shift(step):
        return jnp.where(forward, step, groups - step)

    raw_target = lax.rem(group + key_shift(RAW), groups)
    before = lax.rem(group + groups - RAW, groups)
    after = lax.rem(group + RAW, groups)
    raw_before = (before < duos) & (lax.rem(before, 2) == 1)
    raw_after = (after >= duos) & (lax.rem(after, 2) == 0)
    receiver = raw_before | raw_after
    plain = jnp.logical_not(receiver)

    bunch = groups // BUNCHES
    span = 2 * block * bunch

    def token_copy(j):
        columns = pl.ds(pl.multiple_of(j * span, span), span)
        return pltpu.make_async_copy(
            tokens_hbm.at[:, columns], tokens.at[:, columns], token_sem.at[j]
        )

    def load(which, split):
        source = key_hbm if which == 0 else value_hbm
        columns = pl.ds(split * width, width)
        return pltpu.make_async_copy(
            source.at[:, columns], cotangents.at[which, :, columns], load_sem.at[which, split]
        )

    first = jnp.where(inner, lax.div(raw_target, bunch), 0)

    def order(k):
        return lax.rem(first + k, BUNCHES)

    token_copy(order(0)).start()
    for split in range(SPLITS):
        load(0, split).start()

    @pl.loop(1, replicas * shard_count)
    def _(slot):
        peer = (
            lax.rem(shard + lax.div(slot, replicas), shard_count),
            lax.rem(rep + lax.rem(slot, replicas), replicas),
        )
        pl.semaphore_signal(barrier, inc=1, device_id=peer, device_id_type=MESH)

    def remote(source, target, send_sem, recv_sem, peer):
        return pltpu.make_async_remote_copy(
            src_ref=source, dst_ref=target, send_sem=send_sem, recv_sem=recv_sem,
            device_id=(shard, peer), device_id_type=MESH,
        )

    def tensor(which):
        return (key_full, key_other) if which == 0 else (value_full, value_other)

    def place(split):
        return pl.ds(split * width, width)

    def swap(which, at, split):
        full, other = tensor(which)
        these = pl.ds(at * bunch, bunch)
        return remote(
            full.at[these, 1 - core, :, place(split)], other.at[these, :, place(split)],
            swap_send.at[which, at, split], swap_recv.at[which, at, split], rep + 1 - 2 * core,
        )

    def multiply(which, at, split):
        full = tensor(which)[0]
        left = tokens[:, pl.ds(pl.multiple_of(at * span, span), span)]
        product = lax.dot_general(
            left, cotangents[which, :, place(split)], (((0,), (0,)), ((), ())),
            preferred_element_type=jnp.float32,
        ) * factor
        for j in range(bunch):
            for side in range(2):
                begin = (2 * j + side) * block
                full[at * bunch + j, side, :, place(split)] = product[begin : begin + block]

    def duel(left, right, sums):
        products = (left * right, left * left, right * right)
        return tuple(s + fold(p) for s, p in zip(sums, products))

    def swapped(which, at, split, sums):
        full, other = tensor(which)
        for j in range(bunch):
            sums = duel(
                full[at * bunch + j, core, :, place(split)], other[at * bunch + j, :, place(split)],
                sums,
            )
        return sums

    def rows(i, size=size):
        return pl.ds(pl.multiple_of(i * size, size), size)

    def over(begin, length, body, start=None):
        if start is None:
            lax.fori_loop(begin // size, (begin + length) // size, lambda i, _: body(rows(i)), None)
            return None
        return lax.fori_loop(
            begin // size, (begin + length) // size, lambda i, c: body(rows(i), c), start
        )

    zero = jnp.zeros((8, LANES), jnp.float32)

    def pair_sums(which, sums):
        for split in range(SPLITS):
            swap(which, order(BUNCHES - 1), split).wait_recv()
            sums = swapped(which, order(BUNCHES - 1), split, sums)
        return [scalar(tile) for tile in sums]

    def pair_places(sums, is_first):
        first, second = sided(is_first, sums[1], sums[2])
        return [(0, sums[0]), (1, first), (2, second)]

    def pair_finish(read):
        squares = (read(1), read(2))
        first, second = pair_coefs(read(0), *squares)
        scale = norm_bound((first, second), squares) / TOP
        own, other = sided(core == 0, first / scale, second / scale)
        return own, other, scale

    def hold(at, values):
        for i, value in enumerate(values):
            held[at + i : at + i + 1, :] = jnp.broadcast_to(value, (1, LANES))

    def holds(at, count):
        return [held[at + i : at + i + 1, 0:1] for i in range(count)]

    def around(span, *scratch):
        return Exchange(span, shard_count, rep, shard, *scratch)

    key_exchange = around(2, key_pay, key_in, kx_s, kx_r)
    value_exchange = around(2, value_pay, value_in, vx_s, vx_r)
    duo_exchange = around(4, duo_pay, duo_in, dx_s, dx_r)
    final_exchange = around(replicas, final_pay, final_in, fx_s, fx_r)

    def key_copy(step, q):
        shift = key_shift(step)
        place = pl.ds(q * part, part)
        return remote(
            key_send.at[shift - 1, place], key_recv.at[shift - 1, place],
            key_ss.at[shift - 1, q], key_rs.at[shift - 1, q],
            2 * lax.rem(group + shift, groups) + core,
        )

    def key_start(step, begin=0, end=parts):
        for q in range(begin, min(end, parts)):
            key_copy(step, q).start()

    def key_encode(step, q=None):
        own, other = holds(0, 2)
        shift = key_shift(step)
        target = lax.rem(group + shift, groups)

        def body(r):
            key_send[shift - 1, r, :] = encode(
                own * key_full[target, core, r, :] + other * key_other[target, r, :]
            )

        over(0 if q is None else q * part, block if q is None else part, body)

    def half_copy(d, q):
        place = pl.ds(q * part, part)
        return remote(
            half_send.at[d, place], half_recv.at[d, place], half_ss.at[d, q], half_rs.at[d, q],
            rep + 2 - 4 * half,
        )

    def last_copy(step, q):
        place = pl.ds(q * part, part)
        target = lax.rem(duo + step, duos)
        return remote(
            last_send.at[step - 1, place], last_recv.at[step - 1, place],
            last_ss.at[step - 1, q], last_rs.at[step - 1, q], rep + 4 * (target - duo),
        )

    far, near = groups - 1, 1
    middle = list(range(groups - 2, 1, -1))
    mixed = [step for step in middle if step != RAW]

    def advance(which, k, sums):
        for split in range(SPLITS):
            swap(which, order(k - 1), split).wait_recv()
            sums = swapped(which, order(k - 1), split, sums)
            multiply(which, order(k), split)
            swap(which, order(k), split).start()
        return sums

    token_copy(order(0)).wait()
    for split in range(SPLITS):
        load(0, split).wait()
        if split == 0:
            token_copy(order(1)).start()
        multiply(0, order(0), split)

    def raw_copy(side):
        return remote(
            raw_send.at[side], raw_recv.at[core], raw_ss.at[side], raw_rs.at[core],
            2 * raw_target + side,
        )

    def raw_weight(side):
        return remote(
            raw_pay.at[side], raw_in.at[core], rw_s.at[side], rw_r.at[core],
            2 * raw_target + side,
        )

    @pl.when(inner)
    def _():
        for side in range(2):
            def body(r, carry, side=side):
                value = key_full[raw_target, side, r, :]
                return carry + fold(value * value)

            square = scalar(over(0, block, body, zero))
            scale = jnp.maximum(jnp.sqrt(square), TINY_BOUND) / TOP
            hold(6 + side, [scale])
            inverse = 1.0 / scale

            def body(r, side=side):
                raw_send[side, r, :] = encode(inverse * key_full[raw_target, side, r, :])

            over(0, block, body)

    pl.semaphore_wait(barrier, replicas * shard_count - 1)
    for split in range(SPLITS):
        swap(0, order(0), split).start()

    @pl.when(inner)
    def _():
        for side in range(2):
            raw_copy(side).start()

    def body(k, sums):
        token_copy(order(k)).wait()

        @pl.when(k < BUNCHES - 1)
        def _():
            token_copy(order(k + 1)).start()

        @pl.when(k == BUNCHES - 1)
        def _():
            for split in range(SPLITS):
                load(1, split).start()

        return advance(0, k, sums)

    sums = lax.fori_loop(1, BUNCHES, body, (zero,) * 3)
    key_exchange.start(pair_places(pair_sums(0, sums), core == 0))
    for split in range(SPLITS):
        load(1, split).wait()
    for split in range(SPLITS):
        multiply(1, order(0), split)
        swap(1, order(0), split).start()

    hold(0, pair_finish(key_exchange.finish()))

    @pl.when(outer)
    def _():
        for q in range(parts):
            key_encode(far, q)
            key_start(far, q, q + 1)

    @pl.when(inner)
    def _():
        own = holds(0, 1)[0]
        for side in range(2):
            weight = own * holds(6 + side, 1)[0]
            raw_pay[side] = jnp.broadcast_to(weight, (1, LANES))
            raw_weight(side).start()
        key_encode(near)
        key_start(near)

    sums = lax.fori_loop(1, BUNCHES, lambda at, sums: advance(1, at, sums), (zero,) * 3)
    value_exchange.start(pair_places(pair_sums(1, sums), core == 0))

    @pl.when(outer)
    def _():
        for step in middle:
            key_encode(step)
            key_start(step, 0, EARLY)
        key_encode(near)

    @pl.when(inner)
    def _():
        for step in mixed:
            key_encode(step)
            key_start(step, 0, EARLY)
        key_encode(far)


    own, other, value_scale = pair_finish(value_exchange.finish())
    hold(3, (own, other, value_scale))

    def half_block(r, d, side):
        j = 2 * d + side
        return own * value_full[j, core, r, :] + other * value_other[j, r, :]

    for d in range(duos):
        for q in range(parts):
            def body(r):
                half_send[d, r, :] = encode(half_block(r, d, 1 - half))

            over(q * part, part, body)
            half_copy(d, q).start()

    @pl.when(outer)
    def _():
        for step in middle:
            key_start(step, EARLY, BEHIND)

    for d in range(duos):
        def body(r):
            value_other[2 * d + half, r, :] = half_block(r, d, half)

        over(0, block, body)

    key_blocks = key_other
    own, other, key_scale = holds(0, 3)

    def body(r, carry):
        value = own * key_full[group, core, r, :] + other * key_other[group, r, :]
        key_blocks[0, r, :] = value
        return carry + fold(value * value)

    key_sums, value_sums = {(0, 0): over(0, block, body, zero)}, {}
    key_ready, value_ready = [0], []

    def absorb(read, blocks, slot, ready, sums, begin, length):
        def body(r, carry):
            value = read(r)
            blocks(slot, r, value)
            others = [blocks(b, r) for b in ready] + [value]
            return tuple(c + fold(value * o) for c, o in zip(carry, others))

        pairs = [(b, slot) for b in ready] + [(slot, slot)]
        start = tuple(sums.get(pair, zero) for pair in pairs)
        sums.update(zip(pairs, over(begin, length, body, start)))

    def key_access(slot, r, value=None):
        if value is None:
            return key_blocks[slot, r, :]
        key_blocks[slot, r, :] = value

    def value_access(slot, r, value=None):
        if value is None:
            return value_full[slot, 0, r, :]
        value_full[slot, 0, r, :] = value

    def key_offset(u):
        return jnp.where(half == 0, u, lax.rem(groups - u, groups))

    def value_offset(u):
        return u

    def key_arrival(u, q):
        shift, place = key_offset(u), pl.ds(q * part, part)
        remote(
            key_send.at[shift - 1, place], key_recv.at[shift - 1, place],
            key_ss.at[shift - 1, q], key_rs.at[shift - 1, q], rep + 1 - 2 * core,
        ).wait_recv()

    def absorb_key(u, q):
        key_arrival(u, q)
        absorb(
            lambda r: decode(key_recv[key_offset(u) - 1, r, :]), key_access, u, key_ready,
            key_sums, q * part, part,
        )

    @pl.when(receiver)
    def _():
        for source in range(2):
            remote(
                raw_send.at[source], raw_recv.at[source], raw_ss.at[source], raw_rs.at[source],
                rep + 1 - 2 * core,
            ).wait_recv()
            remote(
                raw_pay.at[source], raw_in.at[source], rw_s.at[source], rw_r.at[source],
                rep + 1 - 2 * core,
            ).wait_recv()

        def body(r):
            key_blocks[groups - RAW, r, :] = sum(
                raw_in[source][:, :1] * decode(raw_recv[source, r, :]) for source in range(2)
            )

        over(0, block, body)

    for q in range(parts):
        absorb_key(1, q)
    key_ready.append(1)

    duo_sums = (zero,) * 3
    for d in range(duos):
        for q in range(parts):
            half_copy(d, q).wait_recv()

            def body(r, carry):
                left = value_other[2 * d + half, r, :]
                right = decode(half_recv[d, r, :])
                value_other[2 * d + 1 - half, r, :] = right
                return duel(left, right, carry)

            duo_sums = over(q * part, part, body, duo_sums)
    even = half == 0
    places = pair_places([scalar(tile) for tile in duo_sums], even)
    mine = jnp.where(owns(rep, shard, 2), value_scale, 0.0)
    low, high = sided(even, mine, jnp.zeros_like(mine))
    duo_exchange.start(places + [(3, low), (4, high)])

    @pl.when(outer)
    def _():
        for step in middle:
            key_start(step, BEHIND)

    @pl.when(inner)
    def _():
        for step in mixed:
            key_start(step, EARLY)
        key_start(far)

    for at in range(BUNCHES):
        for split in range(SPLITS):
            swap(1, at, split).wait_send()
    read = duo_exchange.finish()
    low, high = read(3), read(4)
    squares = (read(1) * (low * low), read(2) * (high * high))
    first, second = pair_coefs(read(0) * (low * high), *squares)
    duo_scale = norm_bound((first, second), squares) / TOP
    own, other = sided(even, first * low / duo_scale, second * high / duo_scale)

    def duo_block(target, r):
        return (
            own * value_other[2 * target + half, r, :]
            + other * value_other[2 * target + 1 - half, r, :]
        )

    for step in range(1, duos):
        for q in range(parts):
            def body(r):
                last_send[step - 1, r, :] = encode(duo_block(lax.rem(duo + step, duos), r))

            over(q * part, part, body)
            last_copy(step, q).start()

    @pl.when(outer)
    def _():
        key_start(near)

    absorb(lambda r: duo_block(duo, r), value_access, 0, value_ready, value_sums, 0, block)
    value_ready.append(0)
    for u in range(2, groups - 1):
        if u == groups - RAW:
            @pl.when(plain)
            def _():
                for q in range(parts):
                    key_arrival(u, q)

                    def body(r):
                        key_blocks[u, r, :] = decode(key_recv[key_offset(u) - 1, r, :])

                    over(q * part, part, body)

            absorb(
                lambda r: key_blocks[u, r, :], key_access, u, key_ready, key_sums, 0, block
            )
        else:
            for q in range(parts):
                absorb_key(u, q)
        key_ready.append(u)
    for step in range(1, duos):
        for q in range(parts):
            last_copy(step, q).wait_recv()
            absorb(
                lambda r: decode(last_recv[step - 1, r, :]), value_access, step, value_ready,
                value_sums, q * part, part,
            )
            if step == duos - 1:
                absorb_key(groups - 1, q)
        value_ready.append(step)

    key_base, value_base = 0, groups * (groups + 1)
    key_places = [(pair, scalar(tile)) for pair, tile in key_sums.items()]
    value_places = [(pair, scalar(tile)) for pair, tile in value_sums.items()]
    final_exchange.start(
        list(final_places(key_places, groups, 2, key_base, key_scale, rep, shard, key_offset))
        + list(
            final_places(value_places, duos, 4, value_base, duo_scale, rep, shard, value_offset)
        )
    )
    for at in range(BUNCHES):
        for split in range(SPLITS):
            swap(0, at, split).wait_send()
    for step in range(1, groups):
        def drain():
            for q in range(parts):
                key_copy(step, q).wait_send()

        if step == RAW:
            pl.when(outer)(drain)
        else:
            drain()

    @pl.when(inner)
    def _():
        for side in range(2):
            raw_copy(side).wait_send()
            raw_weight(side).wait_send()

    for q in range(parts):
        for d in range(duos):
            half_copy(d, q).wait_send()
        for step in range(1, duos):
            last_copy(step, q).wait_send()
    read = final_exchange.finish()
    key_weights = list(final_weights(read, groups, 2, key_base, rep, key_offset))
    value_weights = list(final_weights(read, duos, 4, value_base, rep, value_offset))
    for i, weight in enumerate(key_weights + value_weights):
        wide[i : i + 1, :] = jnp.broadcast_to(weight, (1, features))

    def body(r):
        key_out[r, :] = sum(wide[i : i + 1, :] * key_blocks[i, r, :] for i in range(groups))
        value_out[r, :] = sum(
            wide[groups + i : groups + i + 1, :] * value_full[i, 0, r, :] for i in range(duos)
        )

    over(0, block, body)


def shards(
    tokens, key_cotangent, value_cotangent, key_weight, value_weight, key_moment, value_moment
):
    replicas, shard_count = lax.axis_size("rep"), lax.axis_size("shard")
    depth, width = tokens.shape
    features = key_cotangent.shape[1]
    groups, duos = replicas // 2, replicas // 4
    block = width // replicas
    f32, dma = jnp.float32, pltpu.SemaphoreType.DMA
    entries = groups * (groups + 1) + duos * (duos + 1)
    lines = -(-entries // LANES)

    def small(span, lines=1):
        return [
            pltpu.VMEM((lines, LANES), f32),
            pltpu.VMEM((span * shard_count, lines, LANES), f32),
        ]

    def coded(count):
        return [pltpu.VMEM((max(count, 1), block, features), CODE)] * 2

    def pair(*shape):
        return [dma(shape)] * 2

    parts = min(PARTS, block // 16)
    scratch = [
        pltpu.VMEM((depth, width), tokens.dtype),
        pltpu.VMEM((2, depth, features), key_cotangent.dtype),
        pltpu.VMEM((groups, 2, block, features), f32),
        pltpu.VMEM((groups, 2, block, features), f32),
        pltpu.VMEM((groups, block, features), f32),
        pltpu.VMEM((groups, block, features), f32),
        *coded(groups - 1), *coded(duos), *coded(duos - 1), *coded(2),
        pltpu.VMEM((8, LANES), f32),
        pltpu.VMEM((groups + duos, features), f32),
        pltpu.VMEM((2, 1, LANES), f32), pltpu.VMEM((2, 1, LANES), f32),
        *small(2), *small(2), *small(4), *small(replicas, lines),
        dma((BUNCHES,)), dma((2, SPLITS)), *pair(2, BUNCHES, SPLITS),
        *pair(groups - 1, parts), *pair(duos, parts), *pair(max(duos - 1, 1), parts),
        *pair(2), *pair(2),
        *pair(2 * shard_count), *pair(2 * shard_count), *pair(4 * shard_count),
        *pair(replicas * shard_count),
    ]
    key_merged, value_merged = pl.pallas_call(
        functools.partial(merge_kernel, replicas, shard_count),
        out_shape=[pltpu.VMEM((block, features), f32)] * 2,
        in_specs=[pl.BlockSpec(memory_space=pl.ANY)] * 3,
        out_specs=[pl.BlockSpec(memory_space=pltpu.VMEM)] * 2,
        scratch_shapes=scratch,
        compiler_params=pltpu.CompilerParams(
            collective_id=0, has_side_effects=True, vmem_limit_bytes=VMEM_LIMIT
        ),
    )(tokens, key_cotangent, value_cotangent)
    new_key_moment = MOMENTUM_DECAY * key_moment + key_merged
    new_value_moment = MOMENTUM_DECAY * value_moment + value_merged
    new_key_weight = key_weight - STEP_SIZE * new_key_moment
    new_value_weight = value_weight - STEP_SIZE * new_value_moment
    return new_key_weight, new_value_weight, new_key_moment, new_value_moment


def solution(mesh):
    grads = (P("rep", None),) * 2
    rows = (P(("shard", "rep"), None),) * 4
    return jax.shard_map(
        shards, mesh=mesh, in_specs=(P("rep", "shard"),) + grads + rows, out_specs=rows,
        check_vma=False,
    )
```

time: 136 us -> 109 us (0.80)
  Pallas kernels: 129 us -> 105 us
  local copies, waits for them, and re-layouts: 6.71 us -> 0.02 us
  other arithmetic: 0 us -> 2.68 us
    pallas_call x1, Pallas kernels: 129 us -> 105 us  [shards(): pl.pallas_call(functools.partial(merge_kernel, replicas, shard_count), ou...]
    unnamed x8, local copies, waits for them, and re-layouts: 6.71 us -> 0.02 us
    sub x0 -> x1, other arithmetic: none -> 2.68 us  [shards(): new_value_weight = value_weight - STEP_SIZE * new_value_moment]
where the time goes in v1:
time: 109 us
  Pallas kernels  105 us (96%)
  other arithmetic  2.68 us (2%)
    pallas_call x1, Pallas kernels, shards(): pl.pallas_call(functools.partial(merge_kernel, replicas, shard_count), ou...  105 us
    sub x1, other arithmetic, shards(): new_value_weight = value_weight - STEP_SIZE * new_value_moment  2.68 us

profile of v1, /device:TPU:0, one launch (start us, length us, event | category | flops | bytes accessed | tf_op | source)
XLA Modules:
  0.0 108.8 jit_solution(8542283039116197587)
XLA Ops:
  0.6 0.0 copy-start.1
  0.6 0.0 copy-start.3
  0.7 0.0 copy-start
  0.7 0.0 copy-start.2
  0.7 105.4 %shard_map.102 = (f32[256,1024]{1,0:T(8,128)S(1)}, f32[256,1024]{1,0:T(8,128)S(1)}) custom-call(bf16[2048,2048]{1,0:T(8,128)(2,1)} %refs_0_.1, bf16[2048,1024]{1,0:T(8,128)(2,1)} %refs_1_.1, bf16[2048,1024]{1,0:T(8,128)(2,1)} %refs_2_.1), custom_call_target="tpu_custom_call" | custom-call | tf_op jit(solution)/shard_map/pallas_call | solution.py:779
  106.1 0.0 copy-done.1
  106.1 0.0 copy-done.3
  106.1 0.0 copy-done
  106.1 0.0 copy-done.2
  106.1 2.7 %multiply_subtract_fusion = (f32[256,1024]{1,0:T(8,128)}, f32[256,1024]{1,0:T(8,128)}, f32[256,1024]{1,0:T(8,128)}, f32[256,1024]{1,0:T(8,128)}) fusion(f32[256,1024]{1,0:T(8,128)S(1)} %copy-done, f32[256,1024]{1,0:T(8,128)S(1)} %get-tuple-element.7, f32[256,1024]{1,0:T(8,128)S(1)} %copy-done.1, f32[256,1024]{1,0:T(8,128)S(1)} %copy-done.2, ...), kind=kLoop, calls=%fused_computation | loop fusion | flops 2097152 | bytes 10485760 | tf_op jit(solution)/shard_map/sub | solution.py:792
Async XLA Ops:
  0.6 105.5 %copy-start.1 = (f32[256,1024]{1,0:T(8,128)S(1)}, f32[256,1024]{1,0:T(8,128)}, u32[]{:S(2)}) copy-start(f32[256,1024]{1,0:T(8,128)} %param.13) | copy-start | bytes 3145732
  0.6 105.5 %copy-start.3 = (f32[256,1024]{1,0:T(8,128)S(1)}, f32[256,1024]{1,0:T(8,128)}, u32[]{:S(2)}) copy-start(f32[256,1024]{1,0:T(8,128)} %param.12) | copy-start | bytes 3145732
  0.7 105.5 %copy-start = (f32[256,1024]{1,0:T(8,128)S(1)}, f32[256,1024]{1,0:T(8,128)}, u32[]{:S(2)}) copy-start(f32[256,1024]{1,0:T(8,128)} %param.11) | copy-start | bytes 3145732
  0.7 105.5 %copy-start.2 = (f32[256,1024]{1,0:T(8,128)S(1)}, f32[256,1024]{1,0:T(8,128)}, u32[]{:S(2)}) copy-start(f32[256,1024]{1,0:T(8,128)} %param.10) | copy-start | bytes 3145732

commit v2 on v1

--- a/solution.py
+++ b/solution.py
@@ -21,9 +21,10 @@
 PARTS = 4
 BUNCHES = 4
 SPLITS = 2
-EARLY = 0
+EARLY = 1
 BEHIND = 3
 RAW = 2
+RAW_PARTS = 3
 VMEM_LIMIT = 54 * 2**20
 
 
@@ -99,6 +100,11 @@
     return jnp.sum(jnp.sum(tile, axis=0, keepdims=True), axis=1, keepdims=True)
 
 
+def wrapped(position, shift, size):
+    moved = position + shift
+    return jnp.where(moved >= size, moved - size, moved)
+
+
 class Exchange:
     def __init__(self, span, shard_count, rep, shard, payload, inbox, send_sem, recv_sem):
         self.span, self.shard_count, self.rep, self.shard = span, shard_count, rep, shard
@@ -106,39 +112,33 @@
         self.send_sem, self.recv_sem = send_sem, recv_sem
         self.shape = payload.shape
 
-    def copy(self, slot):
-        inside = lax.rem(self.rep, self.span)
-        near, far = lax.rem(slot, self.span), lax.div(slot, self.span)
-        target = self.rep - inside + lax.rem(inside + near, self.span)
-        return pltpu.make_async_remote_copy(
-            src_ref=self.payload,
-            dst_ref=self.inbox.at[slot],
-            send_sem=self.send_sem.at[slot],
-            recv_sem=self.recv_sem.at[slot],
-            device_id=(lax.rem(self.shard + far, self.shard_count), target),
-            device_id_type=MESH,
-        )
-
     def start(self, placed):
         flat = lax.broadcasted_iota(jnp.int32, self.shape, 0) * LANES
         flat = flat + lax.broadcasted_iota(jnp.int32, self.shape, 1)
-        tile = jnp.zeros(self.shape, jnp.float32)
-        for place, value in placed:
-            tile = jnp.where(flat == place, value, tile)
-        self.payload[...] = tile
-
-        @pl.loop(1, self.span * self.shard_count)
-        def _(slot):
-            self.copy(slot).start()
+        tiles = [jnp.where(flat == place, value, 0.0) for place, value in placed]
+        self.payload[...] = tree_sum(tiles)
+        inside = lax.rem(self.rep, self.span)
+        nears = [self.rep - inside + wrapped(inside, i, self.span) for i in range(self.span)]
+        fars = [wrapped(self.shard, i, self.shard_count) for i in range(self.shard_count)]
+        for near in sorted(range(self.span), key=lambda n: -min(n, self.span - n)):
+            for far in reversed(range(self.shard_count)):
+                if near or far:
+                    pltpu.make_async_remote_copy(
+                        src_ref=self.payload,
+                        dst_ref=self.inbox.at[far * self.span + near - 1],
+                        send_sem=self.send_sem,
+                        recv_sem=self.recv_sem,
+                        device_id=(fars[far], nears[near]),
+                        device_id_type=MESH,
+                    ).start()
+
+    def all_copies(self, sem):
+        return pltpu.make_async_copy(self.inbox, self.inbox, sem)
 
     def finish(self):
-        @pl.loop(1, self.span * self.shard_count)
-        def _(slot):
-            self.copy(slot).wait()
-
-        total = self.payload[...]
-        for slot in range(1, self.span * self.shard_count):
-            total = total + self.inbox[slot]
+        self.all_copies(self.recv_sem).wait()
+        count = self.span * self.shard_count - 1
+        total = tree_sum([self.payload[...]] + [self.inbox[slot] for slot in range(count)])
 
         def read(place):
             line, lane = place // LANES, place % LANES
@@ -146,6 +146,9 @@
             return (pltpu.roll(row, LANES - lane, 1) if lane else row)[:, :1]
 
         return read
+
+    def drain(self):
+        self.all_copies(self.send_sem).wait()
 
 
 def owns(rep, shard, members):
@@ -200,6 +203,8 @@
     size = min(block, ROWS)
     parts = min(PARTS, block // 16)
     part = block // parts
+    raw_parts = min(RAW_PARTS, parts)
+    raw_rows = raw_parts * part
     barrier = pltpu.get_barrier_semaphore()
 
     forward = group < duos
@@ -242,13 +247,14 @@
     for split in range(SPLITS):
         load(0, split).start()
 
-    @pl.loop(1, replicas * shard_count)
-    def _(slot):
-        peer = (
-            lax.rem(shard + lax.div(slot, replicas), shard_count),
-            lax.rem(rep + lax.rem(slot, replicas), replicas),
-        )
-        pl.semaphore_signal(barrier, inc=1, device_id=peer, device_id_type=MESH)
+    nears = [wrapped(rep, i, replicas) for i in range(replicas)]
+    fars = [wrapped(shard, i, shard_count) for i in range(shard_count)]
+    for near in range(replicas):
+        for far in range(shard_count):
+            if near or far:
+                pl.semaphore_signal(
+                    barrier, inc=1, device_id=(fars[far], nears[near]), device_id_type=MESH
+                )
 
     def remote(source, target, send_sem, recv_sem, peer):
         return pltpu.make_async_remote_copy(
@@ -400,8 +406,9 @@
         multiply(0, order(0), split)
 
     def raw_copy(side):
+        these = pl.ds(0, raw_rows)
         return remote(
-            raw_send.at[side], raw_recv.at[core], raw_ss.at[side], raw_rs.at[core],
+            raw_send.at[side, these], raw_recv.at[core, these], raw_ss.at[side], raw_rs.at[core],
             2 * raw_target + side,
         )
 
@@ -418,7 +425,7 @@
                 value = key_full[raw_target, side, r, :]
                 return carry + fold(value * value)
 
-            square = scalar(over(0, block, body, zero))
+            square = scalar(over(0, raw_rows, body, zero))
             scale = jnp.maximum(jnp.sqrt(square), TINY_BOUND) / TOP
             hold(6 + side, [scale])
             inverse = 1.0 / scale
@@ -426,7 +433,7 @@
             def body(r, side=side):
                 raw_send[side, r, :] = encode(inverse * key_full[raw_target, side, r, :])
 
-            over(0, block, body)
+            over(0, raw_rows, body)
 
     pl.semaphore_wait(barrier, replicas * shard_count - 1)
     for split in range(SPLITS):
@@ -474,6 +481,9 @@
             weight = own * holds(6 + side, 1)[0]
             raw_pay[side] = jnp.broadcast_to(weight, (1, LANES))
             raw_weight(side).start()
+        for q in range(raw_parts, parts):
+            key_encode(RAW, q)
+        key_start(RAW, raw_parts)
         key_encode(near)
         key_start(near)
 
@@ -576,9 +586,10 @@
     @pl.when(receiver)
     def _():
         for source in range(2):
+            these = pl.ds(0, raw_rows)
             remote(
-                raw_send.at[source], raw_recv.at[source], raw_ss.at[source], raw_rs.at[source],
-                rep + 1 - 2 * core,
+                raw_send.at[source, these], raw_recv.at[source, these], raw_ss.at[source],
+                raw_rs.at[source], rep + 1 - 2 * core,
             ).wait_recv()
             remote(
                 raw_pay.at[source], raw_in.at[source], rw_s.at[source], rw_r.at[source],
@@ -590,7 +601,7 @@
                 raw_in[source][:, :1] * decode(raw_recv[source, r, :]) for source in range(2)
             )
 
-        over(0, block, body)
+        over(0, raw_rows, body)
 
     for q in range(parts):
         absorb_key(1, q)
@@ -657,9 +668,8 @@
     value_ready.append(0)
     for u in range(2, groups - 1):
         if u == groups - RAW:
-            @pl.when(plain)
-            def _():
-                for q in range(parts):
+            def unpack(begin, end):
+                for q in range(begin, end):
                     key_arrival(u, q)
 
                     def body(r):
@@ -667,6 +677,8 @@
 
                     over(q * part, part, body)
 
+            pl.when(plain)(lambda: unpack(0, raw_parts))
+            unpack(raw_parts, parts)
             absorb(
                 lambda r: key_blocks[u, r, :], key_access, u, key_ready, key_sums, 0, block
             )
@@ -698,14 +710,15 @@
         for split in range(SPLITS):
             swap(0, at, split).wait_send()
     for step in range(1, groups):
-        def drain():
-            for q in range(parts):
+        def drain(begin, end, step=step):
+            for q in range(begin, end):
                 key_copy(step, q).wait_send()
 
         if step == RAW:
-            pl.when(outer)(drain)
+            pl.when(outer)(lambda: drain(0, raw_parts))
+            drain(raw_parts, parts)
         else:
-            drain()
+            drain(0, parts)
 
     @pl.when(inner)
     def _():
@@ -718,6 +731,8 @@
             half_copy(d, q).wait_send()
         for step in range(1, duos):
             last_copy(step, q).wait_send()
+    for exchange in (key_exchange, value_exchange, duo_exchange):
+        exchange.drain()
     read = final_exchange.finish()
     key_weights = list(final_weights(read, groups, 2, key_base, rep, key_offset))
     value_weights = list(final_weights(read, duos, 4, value_base, rep, value_offset))
@@ -731,6 +746,7 @@
         )
 
     over(0, block, body)
+    final_exchange.drain()
 
 
 def shards(
@@ -748,7 +764,7 @@
     def small(span, lines=1):
         return [
             pltpu.VMEM((lines, LANES), f32),
-            pltpu.VMEM((span * shard_count, lines, LANES), f32),
+            pltpu.VMEM((span * shard_count - 1, lines, LANES), f32),
         ]
 
     def coded(count):
@@ -773,8 +789,7 @@
         dma((BUNCHES,)), dma((2, SPLITS)), *pair(2, BUNCHES, SPLITS),
         *pair(groups - 1, parts), *pair(duos, parts), *pair(max(duos - 1, 1), parts),
         *pair(2), *pair(2),
-        *pair(2 * shard_count), *pair(2 * shard_count), *pair(4 * shard_count),
-        *pair(replicas * shard_count),
+        *[dma] * 8,
     ]
     key_merged, value_merged = pl.pallas_call(
         functools.partial(merge_kernel, replicas, shard_count),

time: 109 us -> 106 us (0.972)
  Pallas kernels: 105 us -> 103 us
    pallas_call x1, Pallas kernels: 105 us -> 103 us  [shards(): pl.pallas_call(functools.partial(merge_kernel, replicas, shard_count), ou...]
where the time goes in v2:
time: 106 us
  Pallas kernels  103 us (97%)
  other arithmetic  2.68 us (3%)
    pallas_call x1, Pallas kernels, shards(): pl.pallas_call(functools.partial(merge_kernel, replicas, shard_count), ou...  103 us
    sub x1, other arithmetic, shards(): new_value_weight = value_weight - STEP_SIZE * new_value_moment  2.68 us

profile of v2, /device:TPU:0, one launch (start us, length us, event | category | flops | bytes accessed | tf_op | source)
XLA Modules:
  0.0 106.0 jit_solution(4710768290684587624)
XLA Ops:
  0.6 0.0 copy-start.1
  0.6 0.0 copy-start.3
  0.7 0.0 copy-start
  0.7 0.0 copy-start.2
  0.7 102.6 %shard_map.102 = (f32[256,1024]{1,0:T(8,128)S(1)}, f32[256,1024]{1,0:T(8,128)S(1)}) custom-call(bf16[2048,2048]{1,0:T(8,128)(2,1)} %refs_0_.1, bf16[2048,1024]{1,0:T(8,128)(2,1)} %refs_1_.1, bf16[2048,1024]{1,0:T(8,128)(2,1)} %refs_2_.1), custom_call_target="tpu_custom_call" | custom-call | tf_op jit(solution)/shard_map/pallas_call | solution.py:794
  103.3 0.0 copy-done.1
  103.3 0.0 copy-done.3
  103.3 0.0 copy-done
  103.3 0.0 copy-done.2
  103.3 2.7 %multiply_subtract_fusion = (f32[256,1024]{1,0:T(8,128)}, f32[256,1024]{1,0:T(8,128)}, f32[256,1024]{1,0:T(8,128)}, f32[256,1024]{1,0:T(8,128)}) fusion(f32[256,1024]{1,0:T(8,128)S(1)} %copy-done, f32[256,1024]{1,0:T(8,128)S(1)} %get-tuple-element.7, f32[256,1024]{1,0:T(8,128)S(1)} %copy-done.1, f32[256,1024]{1,0:T(8,128)S(1)} %copy-done.2, ...), kind=kLoop, calls=%fused_computation | loop fusion | flops 2097152 | bytes 10485760 | tf_op jit(solution)/shard_map/sub | solution.py:807
Async XLA Ops:
  0.6 102.6 %copy-start.1 = (f32[256,1024]{1,0:T(8,128)S(1)}, f32[256,1024]{1,0:T(8,128)}, u32[]{:S(2)}) copy-start(f32[256,1024]{1,0:T(8,128)} %param.13) | copy-start | bytes 3145732
  0.6 102.6 %copy-start.3 = (f32[256,1024]{1,0:T(8,128)S(1)}, f32[256,1024]{1,0:T(8,128)}, u32[]{:S(2)}) copy-start(f32[256,1024]{1,0:T(8,128)} %param.12) | copy-start | bytes 3145732
  0.7 102.6 %copy-start = (f32[256,1024]{1,0:T(8,128)S(1)}, f32[256,1024]{1,0:T(8,128)}, u32[]{:S(2)}) copy-start(f32[256,1024]{1,0:T(8,128)} %param.11) | copy-start | bytes 3145732
  0.7 102.6 %copy-start.2 = (f32[256,1024]{1,0:T(8,128)S(1)}, f32[256,1024]{1,0:T(8,128)}, u32[]{:S(2)}) copy-start(f32[256,1024]{1,0:T(8,128)} %param.10) | copy-start | bytes 3145732

commit v3 on v2

--- a/solution.py
+++ b/solution.py
@@ -17,12 +17,12 @@
 CODE = jnp.bfloat16
 MESH = pl.DeviceIdType.MESH
 LANES = 128
-ROWS = 32
+ROWS = 64
 PARTS = 4
 BUNCHES = 4
 SPLITS = 2
 EARLY = 1
-BEHIND = 3
+BEHIND = 4
 RAW = 2
 RAW_PARTS = 3
 VMEM_LIMIT = 54 * 2**20
@@ -200,9 +200,9 @@
     block, features = key_other.shape[1], key_other.shape[2]
     width = features // SPLITS
     factor = 1.0 / math.sqrt(tokens.shape[0])
-    size = min(block, ROWS)
     parts = min(PARTS, block // 16)
     part = block // parts
+    size = min(part, ROWS)
     raw_parts = min(RAW_PARTS, parts)
     raw_rows = raw_parts * part
     barrier = pltpu.get_barrier_semaphore()

time: 106 us -> 106 us (level)
  no operation moved by 1% of the time
where the time goes in v3:
time: 106 us
  Pallas kernels  102 us (96%)
  other arithmetic  2.68 us (3%)
    pallas_call x1, Pallas kernels, shards(): pl.pallas_call(functools.partial(merge_kernel, replicas, shard_count), ou...  102 us
    sub x1, other arithmetic, shards(): new_value_weight = value_weight - STEP_SIZE * new_value_moment  2.68 us

profile of v3, /device:TPU:0, one launch (start us, length us, event | category | flops | bytes accessed | tf_op | source)
XLA Modules:
  0.0 105.7 jit_solution(8731559883611213220)
XLA Ops:
  0.6 0.0 copy-start.1
  0.6 0.0 copy-start.3
  0.7 0.0 copy-start
  0.7 0.0 copy-start.2
  0.7 102.3 %shard_map.102 = (f32[256,1024]{1,0:T(8,128)S(1)}, f32[256,1024]{1,0:T(8,128)S(1)}) custom-call(bf16[2048,2048]{1,0:T(8,128)(2,1)} %refs_0_.1, bf16[2048,1024]{1,0:T(8,128)(2,1)} %refs_1_.1, bf16[2048,1024]{1,0:T(8,128)(2,1)} %refs_2_.1), custom_call_target="tpu_custom_call" | custom-call | tf_op jit(solution)/shard_map/pallas_call | solution.py:794
  103.0 0.0 copy-done.1
  103.0 0.0 copy-done.3
  103.0 0.0 copy-done
  103.0 0.0 copy-done.2
  103.0 2.7 %multiply_subtract_fusion = (f32[256,1024]{1,0:T(8,128)}, f32[256,1024]{1,0:T(8,128)}, f32[256,1024]{1,0:T(8,128)}, f32[256,1024]{1,0:T(8,128)}) fusion(f32[256,1024]{1,0:T(8,128)S(1)} %copy-done, f32[256,1024]{1,0:T(8,128)S(1)} %get-tuple-element.7, f32[256,1024]{1,0:T(8,128)S(1)} %copy-done.1, f32[256,1024]{1,0:T(8,128)S(1)} %copy-done.2, ...), kind=kLoop, calls=%fused_computation | loop fusion | flops 2097152 | bytes 10485760 | tf_op jit(solution)/shard_map/sub | solution.py:807
Async XLA Ops:
  0.6 102.3 %copy-start.1 = (f32[256,1024]{1,0:T(8,128)S(1)}, f32[256,1024]{1,0:T(8,128)}, u32[]{:S(2)}) copy-start(f32[256,1024]{1,0:T(8,128)} %param.13) | copy-start | bytes 3145732
  0.6 102.3 %copy-start.3 = (f32[256,1024]{1,0:T(8,128)S(1)}, f32[256,1024]{1,0:T(8,128)}, u32[]{:S(2)}) copy-start(f32[256,1024]{1,0:T(8,128)} %param.12) | copy-start | bytes 3145732
  0.7 102.3 %copy-start = (f32[256,1024]{1,0:T(8,128)S(1)}, f32[256,1024]{1,0:T(8,128)}, u32[]{:S(2)}) copy-start(f32[256,1024]{1,0:T(8,128)} %param.11) | copy-start | bytes 3145732
  0.7 102.3 %copy-start.2 = (f32[256,1024]{1,0:T(8,128)S(1)}, f32[256,1024]{1,0:T(8,128)}, u32[]{:S(2)}) copy-start(f32[256,1024]{1,0:T(8,128)} %param.10) | copy-start | bytes 3145732
